TPU v7x, 32 devices: a whole 2x2x4 slice. The times are simulated.
32 devices in a mesh: dp: 8 (over y, x, core), tensor: 4 (over z).
Axes of the slice: x: 2, y: 2, z: 4, core: 2. Of those that a mesh axis runs over, the one named last changes fastest.
Arguments:
- tokens: bfloat16 [8, 736, 1152], P('dp', 'tensor'), may hold values from -45 to 45
- key_mask: int32 [8, 736], P('dp'), may hold values from 0 to 1, as said below
- query_weight: bfloat16 [1152, 1152], P('dp', 'tensor'), may hold values from -0.1875 to 0.1875
- key_weight: bfloat16 [1152, 1152], P('dp', 'tensor'), may hold values from -0.1875 to 0.1875
- value_weight: bfloat16 [1152, 1152], P('dp', 'tensor'), may hold values from -0.1875 to 0.1875
- out_weight: bfloat16 [1152, 1152], P('tensor', 'dp'), may hold values from -0.375 to 0.375
- up_weight: bfloat16 [1152, 4304], P('dp', 'tensor'), may hold values from -0.1875 to 0.1875
- down_weight: bfloat16 [4304, 1152], P('tensor', 'dp'), may hold values from -0.09375 to 0.09375
- first_gain: bfloat16 [1152], P('dp'), may hold values from 0.5 to 1.5
- first_shift: bfloat16 [1152], P('dp'), may hold values from -3 to 3
- query_bias: bfloat16 [1152], P('dp'), may hold values from -3 to 3
- value_bias: bfloat16 [1152], P('dp'), may hold values from -3 to 3
- out_bias: bfloat16 [1152], P('dp'), may hold values from -3 to 3
- second_gain: bfloat16 [1152], P('dp'), may hold values from 0.5 to 1.5
- second_shift: bfloat16 [1152], P('dp'), may hold values from -3 to 3
- up_bias: bfloat16 [4304], P('dp'), may hold values from -3 to 3
- down_bias: bfloat16 [1152], P('dp'), may hold values from -3 to 3
- cotangent: bfloat16 [8, 736, 1152], P('dp', 'tensor'), may hold values from -6 to 6
Outputs:
- output: bfloat16 [8, 736, 1152], P('dp', 'tensor')
- input_grad: float32 [8, 736, 1152], P('dp', 'tensor')
- query_grad: float32 [1152, 1152], P('dp', 'tensor')
- key_grad: float32 [1152, 1152], P('dp', 'tensor')
- value_grad: float32 [1152, 1152], P('dp', 'tensor')
- out_grad: float32 [1152, 1152], P('tensor', 'dp')
- up_grad: float32 [1152, 4304], P('dp', 'tensor')
- down_grad: float32 [4304, 1152], P('tensor', 'dp')
- first_gain_grad: float32 [1152], P('dp')
- first_shift_grad: float32 [1152], P('dp')
- query_bias_grad: float32 [1152], P('dp')
- value_bias_grad: float32 [1152], P('dp')
- out_bias_grad: float32 [1152], P('dp')
- second_gain_grad: float32 [1152], P('dp')
- second_shift_grad: float32 [1152], P('dp')
- up_bias_grad: float32 [4304], P('dp')
- down_bias_grad: float32 [1152], P('dp')
Inputs may be any that keep to these rules, and one draw needn't show every extreme that they name: `key_mask`: each image's ones form a prefix of its positions, at least its first three quarters.
All inputs are finite; a program needn't handle non-finite values.
Results may differ from a plain program's by a relative error of at most 0.017.
The roundings to bfloat16 on the way count: a program that leaves them out, or rounds other values in their place, can miss the bound.
Values may be sent and summed in bfloat16 or wider, within the bound.
A program may use at most 128 MiB of HBM per device.

v0:
```python
from functools import partial
import math
import jax
import jax.numpy as jnp
from jax import lax
from jax.sharding import PartitionSpec as P

HD = 72
EPSILON = 1e-06
GELU_COEF = 0.7978845608028654
MASK_FILL = -1e30


def norm_forward(inputs, gain_vec, shift_vec):
    centred = inputs - jnp.mean(inputs, axis=-1, keepdims=True)
    inv_std = lax.rsqrt(jnp.mean(centred * centred, axis=-1, keepdims=True) + EPSILON)
    normed = centred * inv_std
    return (normed * gain_vec + shift_vec, normed, inv_std)


def norm_backward(grad_in, normed, inv_std, gain_vec):
    scaled = grad_in * gain_vec
    return inv_std * (
        scaled
        - jnp.mean(scaled, axis=-1, keepdims=True)
        - normed * jnp.mean(scaled * normed, axis=-1, keepdims=True)
    )


def gelu_pair(pre_act):
    tanh_val = jnp.tanh(GELU_COEF * (pre_act + 0.044715 * pre_act * pre_act * pre_act))
    gelu_value = 0.5 * pre_act * (1.0 + tanh_val)
    gelu_slope = 0.5 * (1.0 + tanh_val) + 0.5 * pre_act * (
        1.0 - tanh_val * tanh_val
    ) * GELU_COEF * (1.0 + 3.0 * 0.044715 * pre_act * pre_act)
    return (gelu_value, gelu_slope)


def mat_dot(left, right):
    return jnp.dot(left, right, preferred_element_type=jnp.float32)


def gather_rows(local):
    return lax.all_gather(local, "tensor", axis=1, tiled=True)


def sum_rows(partial_term):
    return lax.psum_scatter(
        partial_term.astype(jnp.bfloat16), "tensor", scatter_dimension=1, tiled=True
    ).astype(jnp.float32)


def attend_image(packed):
    query_img, keys_img, values_img, valid_img = packed
    scores = jnp.einsum("qhd,khd->hqk", query_img, keys_img, preferred_element_type=jnp.float32)
    scores = jnp.where(valid_img[None, None, :] > 0, scores, MASK_FILL)
    highest = jnp.max(scores, axis=-1, keepdims=True)
    logsum = highest + jnp.log(jnp.sum(jnp.exp(scores - highest), axis=-1, keepdims=True))
    probs = jnp.exp(scores - logsum).astype(jnp.bfloat16)
    mixed = jnp.einsum("hqk,khd->qhd", probs, values_img, preferred_element_type=jnp.float32)
    return (mixed.astype(jnp.bfloat16), logsum[..., 0])


def attend_back(scale_factor, packed):
    query_img, keys_img, values_img, valid_img, logsum_img, mixed_img, grad_img = packed
    scores = jnp.einsum("qhd,khd->hqk", query_img, keys_img, preferred_element_type=jnp.float32)
    scores = jnp.where(valid_img[None, None, :] > 0, scores, MASK_FILL)
    probs_full = jnp.exp(scores - logsum_img[:, :, None])
    probs = probs_full.astype(jnp.bfloat16)
    grad_values = jnp.einsum("hqk,qhd->khd", probs, grad_img, preferred_element_type=jnp.float32)
    grad_probs = jnp.einsum(
        "qhd,khd->hqk", grad_img, values_img, preferred_element_type=jnp.float32
    )
    delta = jnp.sum(grad_img.astype(jnp.float32) * mixed_img.astype(jnp.float32), axis=-1).T
    grad_scores = (probs_full * (grad_probs - delta[:, :, None])).astype(jnp.bfloat16)
    grad_query = (
        jnp.einsum("hqk,khd->qhd", grad_scores, keys_img, preferred_element_type=jnp.float32)
        * scale_factor
    )
    grad_keys = jnp.einsum(
        "hqk,qhd->khd", grad_scores, query_img, preferred_element_type=jnp.float32
    )
    return (grad_query, grad_keys, grad_values)


def vector_share(full_vec, parts, index):
    piece = full_vec.shape[0] // parts
    return lax.dynamic_slice_in_dim(full_vec, index * piece, piece)


def shards(
    tokens,
    key_mask,
    query_weight,
    key_weight,
    value_weight,
    out_weight,
    up_weight,
    down_weight,
    first_gain,
    first_shift,
    query_bias,
    value_bias,
    out_bias,
    second_gain,
    second_shift,
    up_bias,
    down_bias,
    cotangent,
):
    dp_count = lax.axis_size("dp")
    dp_index = lax.axis_index("dp")
    tensor_index = lax.axis_index("tensor")
    images = tokens.shape[0]
    width = tokens.shape[2]
    fetched = (
        lax.all_gather(query_weight, "dp", axis=0, tiled=True),
        lax.all_gather(key_weight, "dp", axis=0, tiled=True),
        lax.all_gather(value_weight, "dp", axis=0, tiled=True),
        lax.all_gather(out_weight, "dp", axis=1, tiled=True),
        lax.all_gather(up_weight, "dp", axis=0, tiled=True),
        lax.all_gather(down_weight, "dp", axis=1, tiled=True),
        lax.all_gather(first_gain, "dp", axis=0, tiled=True),
        lax.all_gather(first_shift, "dp", axis=0, tiled=True),
        lax.all_gather(query_bias, "dp", axis=0, tiled=True),
        lax.all_gather(value_bias, "dp", axis=0, tiled=True),
        lax.all_gather(out_bias, "dp", axis=0, tiled=True),
        lax.all_gather(second_gain, "dp", axis=0, tiled=True),
        lax.all_gather(second_shift, "dp", axis=0, tiled=True),
        lax.all_gather(up_bias, "dp", axis=0, tiled=True),
        lax.all_gather(down_bias, "dp", axis=0, tiled=True),
    )
    query_full, key_full, value_full, out_full, up_full, down_full = fetched[:6]
    (
        gain_one,
        shift_one,
        query_bias_all,
        value_bias_all,
        out_bias_all,
        gain_two,
        shift_two,
        up_bias_all,
        down_bias_all,
    ) = [member.astype(jnp.float32) for member in fetched[6:]]
    head_cols = query_full.shape[1]
    hidden_cols = up_full.shape[1]
    heads_local = head_cols // HD
    query_bias_local = lax.dynamic_slice_in_dim(query_bias_all, tensor_index * head_cols, head_cols)
    value_bias_local = lax.dynamic_slice_in_dim(value_bias_all, tensor_index * head_cols, head_cols)
    up_bias_local = lax.dynamic_slice_in_dim(up_bias_all, tensor_index * hidden_cols, hidden_cols)
    scale_factor = 1.0 / math.sqrt(HD)
    inputs = tokens.astype(jnp.float32)
    first, normed_one, inv_one = norm_forward(inputs, gain_one, shift_one)
    first_rows = gather_rows(first.astype(jnp.bfloat16))
    seq_full = first_rows.shape[1]
    row_shape = (images, seq_full, width)
    head_shape = (images, seq_full, heads_local, HD)
    first_flat = first_rows.reshape(-1, width)
    query = (
        ((mat_dot(first_flat, query_full) + query_bias_local) * scale_factor)
        .astype(jnp.bfloat16)
        .reshape(head_shape)
    )
    keys = mat_dot(first_flat, key_full).astype(jnp.bfloat16).reshape(head_shape)
    values = (
        (mat_dot(first_flat, value_full) + value_bias_local)
        .astype(jnp.bfloat16)
        .reshape(head_shape)
    )
    mixed, logsum = lax.map(attend_image, (query, keys, values, key_mask))
    mixed_flat = mixed.reshape(-1, head_cols)
    hidden = inputs + sum_rows(mat_dot(mixed_flat, out_full).reshape(row_shape)) + out_bias_all
    second, normed_two, inv_two = norm_forward(hidden, gain_two, shift_two)
    second_flat = gather_rows(second.astype(jnp.bfloat16)).reshape(-1, width)
    pre_act = mat_dot(second_flat, up_full) + up_bias_local
    gelu_value, gelu_slope = gelu_pair(pre_act)
    act = gelu_value.astype(jnp.bfloat16)
    output = (hidden + sum_rows(mat_dot(act, down_full).reshape(row_shape)) + down_bias_all).astype(
        jnp.bfloat16
    )
    query_back, key_back, value_back, out_back, up_back, down_back = (
        lax.all_gather(query_weight, "dp", axis=0, tiled=True),
        lax.all_gather(key_weight, "dp", axis=0, tiled=True),
        lax.all_gather(value_weight, "dp", axis=0, tiled=True),
        lax.all_gather(out_weight, "dp", axis=1, tiled=True),
        lax.all_gather(up_weight, "dp", axis=0, tiled=True),
        lax.all_gather(down_weight, "dp", axis=1, tiled=True),
    )
    grad_out = cotangent.astype(jnp.float32)
    down_bias_grad = jnp.sum(grad_out, axis=(0, 1))
    grad_rows = gather_rows(cotangent).reshape(-1, width)
    down_grad = mat_dot(act.T, grad_rows)
    grad_pre = mat_dot(grad_rows, down_back.T) * gelu_slope
    up_bias_part = jnp.sum(grad_pre, axis=0)
    grad_pre_low = grad_pre.astype(jnp.bfloat16)
    up_grad = mat_dot(second_flat.T, grad_pre_low)
    grad_second = sum_rows(mat_dot(grad_pre_low, up_back.T).reshape(row_shape))
    second_gain_grad = jnp.sum(grad_second * normed_two, axis=(0, 1))
    second_shift_grad = jnp.sum(grad_second, axis=(0, 1))
    grad_hidden = grad_out + norm_backward(grad_second, normed_two, inv_two, gain_two)
    out_bias_grad = jnp.sum(grad_hidden, axis=(0, 1))
    hidden_rows = gather_rows(grad_hidden.astype(jnp.bfloat16)).reshape(-1, width)
    grad_mixed = mat_dot(hidden_rows, out_back.T).astype(jnp.bfloat16)
    out_grad = mat_dot(mixed_flat.T, hidden_rows)
    grad_query_f, grad_keys_f, grad_values_f = lax.map(
        partial(attend_back, scale_factor),
        (query, keys, values, key_mask, logsum, mixed, grad_mixed.reshape(head_shape)),
    )
    grad_query_f = grad_query_f.reshape(-1, head_cols)
    grad_keys_f = grad_keys_f.reshape(-1, head_cols)
    grad_values_f = grad_values_f.reshape(-1, head_cols)
    query_bias_part = jnp.sum(grad_query_f, axis=0)
    value_bias_part = jnp.sum(grad_values_f, axis=0)
    grad_query = grad_query_f.astype(jnp.bfloat16)
    grad_keys = grad_keys_f.astype(jnp.bfloat16)
    grad_values = grad_values_f.astype(jnp.bfloat16)
    query_grad = mat_dot(first_flat.T, grad_query)
    key_grad = mat_dot(first_flat.T, grad_keys)
    value_grad = mat_dot(first_flat.T, grad_values)
    first_term = (
        mat_dot(grad_query, query_back.T)
        + mat_dot(grad_keys, key_back.T)
        + mat_dot(grad_values, value_back.T)
    )
    grad_first = sum_rows(first_term.reshape(row_shape))
    first_gain_grad = jnp.sum(grad_first * normed_one, axis=(0, 1))
    first_shift_grad = jnp.sum(grad_first, axis=(0, 1))
    input_grad = grad_hidden + norm_backward(grad_first, normed_one, inv_one, gain_one)
    matrix_shares = (
        lax.psum_scatter(query_grad, "dp", scatter_dimension=0, tiled=True),
        lax.psum_scatter(key_grad, "dp", scatter_dimension=0, tiled=True),
        lax.psum_scatter(value_grad, "dp", scatter_dimension=0, tiled=True),
        lax.psum_scatter(out_grad, "dp", scatter_dimension=1, tiled=True),
        lax.psum_scatter(up_grad, "dp", scatter_dimension=0, tiled=True),
        lax.psum_scatter(down_grad, "dp", scatter_dimension=1, tiled=True),
    )
    query_bias_full = lax.dynamic_update_slice_in_dim(
        jnp.zeros((width,), jnp.float32), query_bias_part, tensor_index * head_cols, 0
    )
    value_bias_full = lax.dynamic_update_slice_in_dim(
        jnp.zeros((width,), jnp.float32), value_bias_part, tensor_index * head_cols, 0
    )
    up_bias_full = lax.dynamic_update_slice_in_dim(
        jnp.zeros((up_bias_all.shape[0],), jnp.float32), up_bias_part, tensor_index * hidden_cols, 0
    )
    vector_sums = lax.psum(
        (
            first_gain_grad,
            first_shift_grad,
            query_bias_full,
            value_bias_full,
            out_bias_grad,
            second_gain_grad,
            second_shift_grad,
            up_bias_full,
            down_bias_grad,
        ),
        ("dp", "tensor"),
    )
    vector_parts = tuple((vector_share(member, dp_count, dp_index) for member in vector_sums))
    return (output, input_grad) + tuple(matrix_shares) + vector_parts


def solution(mesh):
    return jax.shard_map(
        shards,
        mesh=mesh,
        in_specs=(
            P("dp", "tensor", None),
            P("dp", None),
            P("dp", "tensor"),
            P("dp", "tensor"),
            P("dp", "tensor"),
            P("tensor", "dp"),
            P("dp", "tensor"),
            P("tensor", "dp"),
            P("dp"),
            P("dp"),
            P("dp"),
            P("dp"),
            P("dp"),
            P("dp"),
            P("dp"),
            P("dp"),
            P("dp"),
            P("dp", "tensor", None),
        ),
        out_specs=(
            P("dp", "tensor", None),
            P("dp", "tensor", None),
            P("dp", "tensor"),
            P("dp", "tensor"),
            P("dp", "tensor"),
            P("tensor", "dp"),
            P("dp", "tensor"),
            P("tensor", "dp"),
            P("dp"),
            P("dp"),
            P("dp"),
            P("dp"),
            P("dp"),
            P("dp"),
            P("dp"),
            P("dp"),
            P("dp"),
        ),
        check_vma=False,
    )
```

profile of v0, /device:TPU:0, one launch (start us, length us, event | category | flops | bytes accessed | tf_op | source)
XLA Modules:
  0.0 748.6 jit_solution(14068338893583376241)
XLA Ops:
  20.8 26.1 %all-reduce.14 = (bf16[1152]{0:T(1024)(128)(2,1)S(1)}, bf16[1152]{0:T(1024)(128)(2,1)S(1)}, bf16[1152]{0:T(1024)(128)(2,1)S(1)}, bf16[1152]{0:T(1024)(128)(2,1)S...) all-reduce(bf16[1152]{0:T(1024)(128)(2,1)S(1)} %dynamic-update-slic, ...), channel_id=1, replica_groups=mesh['dp'=8,'tensor'=4] {'dp'}, use_global_device_ids=true, to_apply=%add.6 | all-reduce | flops 13520 | bytes 54080
  49.9 10.0 %all_gather.68 = bf16[1152,288]{1,0:T(8,128)(2,1)S(1)} all-gather(bf16[144,288]{1,0:T(8,128)(2,1)} %param.20), channel_id=1, replica_groups=mesh['dp'=8,'tensor'=4] {'dp'}, dimensions={0}, use_global_device_ids=true | all-gather | bytes 746496 | tf_op jit(solution)/shard_map/all_gather | solution.py:117
  59.9 10.5 %all_gather.70 = bf16[1152,288]{1,0:T(8,128)(2,1)S(1)} all-gather(bf16[144,288]{1,0:T(8,128)(2,1)S(1)} %copy-done.18), channel_id=1, replica_groups=mesh['dp'=8,'tensor'=4] {'dp'}, dimensions={0}, use_global_device_ids=true | all-gather | bytes 746496 | tf_op jit(solution)/shard_map/all_gather | solution.py:118
  70.4 10.2 %all_gather.66 = bf16[1152,288]{1,0:T(8,128)(2,1)S(1)} all-gather(bf16[144,288]{1,0:T(8,128)(2,1)S(1)} %copy-done.19), channel_id=1, replica_groups=mesh['dp'=8,'tensor'=4] {'dp'}, dimensions={0}, use_global_device_ids=true | all-gather | bytes 746496 | tf_op jit(solution)/shard_map/all_gather | solution.py:119
  80.5 11.5 %all_gather.71 = bf16[288,1152]{0,1:T(8,128)(2,1)} all-gather(bf16[288,144]{0,1:T(8,128)(2,1)S(1)} %copy-done.20), channel_id=1, replica_groups=mesh['dp'=8,'tensor'=4] {'dp'}, dimensions={1}, use_global_device_ids=true | all-gather | bytes 746496 | tf_op jit(solution)/shard_map/all_gather | solution.py:120
  106.2 37.0 %reduce-scatter.35.cloned.1.call-done = bf16[1,184,1152]{2,1,0:T(8,128)(2,1)} async-done(((bf16[1,736,1152]{2,1,0:T(8,128)(2,1)}), bf16[1,184,1152]{2,1,0:T(8,128)(2,1)}) %reduce-scatter.35.cloned.1.call-update) | async-done | bytes 423952
  149.5 36.8 %all-gather.9.cloned.1.call-done = bf16[1,736,1152]{2,1,0:T(8,128)(2,1)} async-done(((bf16[1,184,1152]{2,1,0:T(8,128)(2,1)}), bf16[1,736,1152]{2,1,0:T(8,128)(2,1)}) %all-gather.9.cloned.1.call-update) | async-done | bytes 1695760 | tf_op jit(solution)/shard_map/all_gather | solution.py:44
  186.3 6.4 convolution_add_fusion.2
  192.8 32.8 %all-gather.15.cloned.1.call-done = bf16[1,736,1152]{2,1,0:T(8,128)(2,1)} async-done(((bf16[1,184,1152]{2,1,0:T(8,128)(2,1)}), bf16[1,736,1152]{2,1,0:T(8,128)(2,1)}) %all-gather.15.cloned.1.call-update) | async-done | bytes 1695760 | tf_op jit(solution)/shard_map/all_gather | solution.py:44
  225.6 30.9 %all-gather.13.cloned.1.call-done = bf16[1076,1152]{0,1:T(8,128)(2,1)} async-done(((bf16[1076,144]{0,1:T(8,128)(2,1)}), bf16[1076,1152]{0,1:T(8,128)(2,1)}) %all-gather.13.cloned.1.call-update) | async-done | bytes 2479120 | tf_op jit(solution)/shard_map/all_gather | solution.py:122
  256.5 8.2 %fusion.86 = (f32[1076]{0:T(1024)}, bf16[736,1076]{0,1:T(8,128)(2,1)S(1)}) fusion(f32[736,1076]{0,1:T(8,128)} %convolution_add_fusion.2, bf16[1076,1152]{0,1:T(8,128)(2,1)} %all-gather.13.cloned.1.call-done, bf16[1,736,1152]{2,1,0:T(8,128)(2,1)} %all-gather.15.cloned.1.call-done), kind=kOutput, calls=%fused_computation.117 | convolution fusion | flops 1840458240 | bytes 8930768 | tf_op jit(solution)/shard_map/dot_general | solution.py:40
  265.9 4.0 fusion.8
  269.9 7.2 fusion.7
  277.2 30.1 %reduce-scatter.39.cloned.1.call-done = bf16[1,184,1152]{2,1,0:T(8,128)(2,1)} async-done(((bf16[1,736,1152]{2,1,0:T(8,128)(2,1)}), bf16[1,184,1152]{2,1,0:T(8,128)(2,1)}) %reduce-scatter.39.cloned.1.call-update) | async-done | bytes 423952
  309.5 36.8 %reduce-scatter.37.cloned.1.call-done = bf16[1,184,1152]{2,1,0:T(8,128)(2,1)} async-done(((bf16[1,736,1152]{2,1,0:T(8,128)(2,1)}), bf16[1,184,1152]{2,1,0:T(8,128)(2,1)}) %reduce-scatter.37.cloned.1.call-update) | async-done | bytes 423952
  350.3 38.2 %all-gather.17.cloned.1.call-done = bf16[1,736,1152]{2,1,0:T(8,128)(2,1)} async-done(((bf16[1,184,1152]{2,1,0:T(8,128)(2,1)}), bf16[1,736,1152]{2,1,0:T(8,128)(2,1)}) %all-gather.17.cloned.1.call-update) | async-done | bytes 1695760 | tf_op jit(solution)/shard_map/all_gather | solution.py:44
  392.1 5.6 fusion.84
  397.8 5.6 multiply_convert_fusion
  410.8 7.4 fusion.15
  419.7 6.5 fusion.18
  427.2 3.9 fusion.11
  431.2 3.9 fusion.21
  435.2 3.9 fusion.25
  439.2 3.8 fusion.23
  444.0 2.7 reduce-scatter.41.cloned.1.call-done
  448.2 41.8 %all-reduce.13 = (f32[1152]{0:T(1024)S(1)}, f32[1152]{0:T(1024)S(1)}, f32[1152]{0:T(1024)S(1)}, f32[1152]{0:T(1024)S(1)}, f32[1152]{0:T(1024)S(1)}, /*index=5*/f...) all-reduce(f32[1152]{0:T(1024)S(1)} %get-tuple-element.73, ...), channel_id=1, replica_groups=mesh['dp'=8,'tensor'=4] {'dp','tensor'}, use_global_device_ids=true, to_apply=%region_22.23 | all-reduce | flops 13520 | bytes 108160 | tf_op jit(solution)/shard_map/psum | solution.py:246
  498.0 9.4 %reduce-scatter.33.cloned.1.call-done = f32[1076,144]{0,1:T(8,128)} async-done(((f32[1076,1152]{0,1:T(8,128)}), f32[1076,144]{0,1:T(8,128)}) %reduce-scatter.33.cloned.1.call-update) | async-done | bytes 619792 | tf_op jit(solution)/shard_map/reduce_scatter | solution.py:235
  507.5 61.1 %reduce-scatter.31.cloned.1.call-done = f32[144,1076]{1,0:T(8,128)} async-done(((f32[1152,1076]{1,0:T(8,128)}), f32[144,1076]{1,0:T(8,128)}) %reduce-scatter.31.cloned.1.call-update) | async-done | bytes 619792 | tf_op jit(solution)/shard_map/reduce_scatter | solution.py:234
  568.5 43.1 %reduce-scatter.29.cloned.1.call-done = f32[288,144]{0,1:T(8,128)} async-done(((f32[288,1152]{0,1:T(8,128)}), f32[288,144]{0,1:T(8,128)}) %reduce-scatter.29.cloned.1.call-update) | async-done | bytes 165904 | tf_op jit(solution)/shard_map/reduce_scatter | solution.py:233
  611.6 43.1 %reduce-scatter.27.cloned.1.call-done = f32[144,288]{1,0:T(8,128)} async-done(((f32[1152,288]{1,0:T(8,128)}), f32[144,288]{1,0:T(8,128)}) %reduce-scatter.27.cloned.1.call-update) | async-done | bytes 165904 | tf_op jit(solution)/shard_map/reduce_scatter | solution.py:232
  654.7 43.3 %reduce-scatter.23.cloned.1.call-done = f32[144,288]{1,0:T(8,128)} async-done(((f32[1152,288]{1,0:T(8,128)}), f32[144,288]{1,0:T(8,128)}) %reduce-scatter.23.cloned.1.call-update) | async-done | bytes 165904 | tf_op jit(solution)/shard_map/reduce_scatter | solution.py:230
  698.0 43.1 %reduce-scatter.25.cloned.1.call-done = f32[144,288]{1,0:T(8,128)} async-done(((f32[1152,288]{1,0:T(8,128)}), f32[144,288]{1,0:T(8,128)}) %reduce-scatter.25.cloned.1.call-update) | async-done | bytes 165904 | tf_op jit(solution)/shard_map/reduce_scatter | solution.py:231
  (173 shorter events, 66.2 us)
Async XLA Ops:
  8.0 51.8 %copy-start.18 = (bf16[144,288]{1,0:T(8,128)(2,1)S(1)}, bf16[144,288]{1,0:T(8,128)(2,1)}, u32[]{:S(2)}) copy-start(bf16[144,288]{1,0:T(8,128)(2,1)} %param.21) | copy-start | bytes 248836
  8.0 62.3 %copy-start.19 = (bf16[144,288]{1,0:T(8,128)(2,1)S(1)}, bf16[144,288]{1,0:T(8,128)(2,1)}, u32[]{:S(2)}) copy-start(bf16[144,288]{1,0:T(8,128)(2,1)} %param.22) | copy-start | bytes 248836
  8.0 72.5 %copy-start.20 = (bf16[288,144]{0,1:T(8,128)(2,1)S(1)}, bf16[288,144]{0,1:T(8,128)(2,1)}, u32[]{:S(2)}) copy-start(bf16[288,144]{0,1:T(8,128)(2,1)} %param.23) | copy-start | bytes 248836
  8.1 84.0 %all-gather.7.cloned.1.call-start = ((), (), s32[]{:S(2)}) async-start(), calls=%async_computation.10 | async-start | bytes 2119680 | tf_op jit(solution)/shard_map/all_gather | solution.py:44
  48.9 94.3 %reduce-scatter.35.cloned.1.call-start = ((), (), s32[]{:S(2)}) async-start(), calls=%async_computation.22 | async-start | bytes 2119680
  70.4 24.9 %copy-start.3 = (bf16[1152,288]{1,0:T(8,128)(2,1)}, bf16[1152,288]{1,0:T(8,128)(2,1)S(1)}, u32[]{:S(2)}) copy-start(bf16[1152,288]{1,0:T(8,128)(2,1)S(1)} %all_gather.70) | copy-start | bytes 1990660
  98.8 3.5 copy-start.21
  102.3 40.9 %copy-start = (bf16[1,184,1152]{2,1,0:T(8,128)(2,1)S(1)}, bf16[1,184,1152]{2,1,0:T(8,128)(2,1)}, u32[]{:S(2)}) copy-start(bf16[1,184,1152]{2,1,0:T(8,128)(2,1)} %param.18) | copy-start | bytes 1271812
  105.5 44.0 %all-gather.11.cloned.1.call-start = ((), (), s32[]{:S(2)}) async-start(), calls=%async_computation.12 | async-start | bytes 2985984 | tf_op jit(solution)/shard_map/all_gather | solution.py:121
  106.1 80.2 %all-gather.9.cloned.1.call-start = ((), (), s32[]{:S(2)}) async-start(), calls=%async_computation.11 | async-start | bytes 2119680 | tf_op jit(solution)/shard_map/all_gather | solution.py:44
  147.8 77.8 %all-gather.15.cloned.1.call-start = ((), (), s32[]{:S(2)}) async-start(), calls=%async_computation.14 | async-start | bytes 2119680 | tf_op jit(solution)/shard_map/all_gather | solution.py:44
  148.4 108.1 %all-gather.13.cloned.1.call-start = ((), (), s32[]{:S(2)}) async-start(), calls=%async_computation.13 | async-start | bytes 2985984 | tf_op jit(solution)/shard_map/all_gather | solution.py:122
  149.1 158.2 %reduce-scatter.39.cloned.1.call-start = ((), (), s32[]{:S(2)}) async-start(), calls=%async_computation.24 | async-start | bytes 2119680
  256.5 9.4 %copy-start.24 = (bf16[1152,1076]{1,0:T(8,128)(2,1)S(1)}, bf16[1152,1076]{1,0:T(8,128)(2,1)}, u32[]{:S(2)}) copy-start(bf16[1152,1076]{1,0:T(8,128)(2,1)} %all-gather.11.cloned.1.call-done) | copy-start | bytes 7437316
  269.9 37.4 %copy-start.2 = (bf16[1,184,1152]{2,1,0:T(8,128)(2,1)S(1)}, bf16[1,184,1152]{2,1,0:T(8,128)(2,1)}, u32[]{:S(2)}) copy-start(bf16[1,184,1152]{2,1,0:T(8,128)(2,1)} %reduce-scatter.35.cloned.1.call-done) | copy-start | bytes 1271812
  269.9 76.4 %reduce-scatter.37.cloned.1.call-start = ((), (), s32[]{:S(2)}) async-start(), calls=%async_computation.23 | async-start | bytes 2119680
  277.2 111.3 %all-gather.17.cloned.1.call-start = ((), (), s32[]{:S(2)}) async-start(), calls=%async_computation.15 | async-start | bytes 2119680 | tf_op jit(solution)/shard_map/all_gather | solution.py:44
  348.9 43.2 %copy-start.22 = (f32[4,736]{1,0:T(4,128)S(1)}, f32[4,736]{1,0:T(4,128)}, u32[]{:S(2)}) copy-start(f32[4,736]{1,0:T(4,128)} %copy-done.21) | copy-start | bytes 35332
  349.8 96.9 %reduce-scatter.41.cloned.1.call-start = ((), (), s32[]{:S(2)}) async-start(), calls=%async_computation.25 | async-start | bytes 2119680
  392.1 5.7 copy-start.28
  397.8 10.6 %copy-start.14 = (bf16[736,4,72]{0,2,1:T(8,128)(2,1)}, bf16[736,4,72]{0,2,1:T(8,128)(2,1)S(1)}, u32[]{:S(2)}) copy-start(bf16[736,4,72]{0,2,1:T(8,128)(2,1)S(1)} %get-tuple-element.100) | copy-start | bytes 1271812
  397.8 5.6 copy-start.10
  410.8 96.7 %reduce-scatter.33.cloned.1.call-start = ((), (), s32[]{:S(2)}) async-start(), calls=%async_computation.21 | async-start | bytes 5971968 | tf_op jit(solution)/shard_map/reduce_scatter | solution.py:235
  418.2 150.3 %reduce-scatter.31.cloned.1.call-start = ((), (), s32[]{:S(2)}) async-start(), calls=%async_computation.20 | async-start | bytes 5971968 | tf_op jit(solution)/shard_map/reduce_scatter | solution.py:234
  426.2 5.0 copy-start.15
  426.2 185.4 %reduce-scatter.29.cloned.1.call-start = ((), (), s32[]{:S(2)}) async-start(), calls=%async_computation.19 | async-start | bytes 1990656 | tf_op jit(solution)/shard_map/reduce_scatter | solution.py:233
  431.1 4.1 copy-start.6
  431.1 223.6 %reduce-scatter.27.cloned.1.call-start = ((), (), s32[]{:S(2)}) async-start(), calls=%async_computation.18 | async-start | bytes 1990656 | tf_op jit(solution)/shard_map/reduce_scatter | solution.py:232
  435.1 4.1 copy-start.12
  435.1 262.8 %reduce-scatter.23.cloned.1.call-start = ((), (), s32[]{:S(2)}) async-start(), calls=%async_computation.16 | async-start | bytes 1990656 | tf_op jit(solution)/shard_map/reduce_scatter | solution.py:230
  439.1 3.9 copy-start.23
  439.1 302.0 %reduce-scatter.25.cloned.1.call-start = ((), (), s32[]{:S(2)}) async-start(), calls=%async_computation.17 | async-start | bytes 1990656 | tf_op jit(solution)/shard_map/reduce_scatter | solution.py:231
  (14 other events, 26.0 us)
Sparse Core Ops, SparseCore 0:
  49.1 38.4 all-gather.6
  105.7 37.5 reduce-scatter.34
  270.0 37.2 reduce-scatter.38
  309.5 36.7 reduce-scatter.36
  349.9 38.5 all-gather.16
Sparse Core Ops, SparseCore 1:
  107.9 30.3 all-gather.10
  147.9 38.4 all-gather.8
  187.8 37.8 all-gather.14
  227.5 28.9 all-gather.12
  410.9 35.8 reduce-scatter.40
  450.7 56.7 reduce-scatter.32
  511.7 56.8 reduce-scatter.30
  572.3 39.2 reduce-scatter.28
  615.4 39.2 reduce-scatter.26
  658.7 39.2 reduce-scatter.22
  701.8 39.2 reduce-scatter.24
where the time goes:
time: 754 us; the launch traced here: 749 us
  waiting for transfers between devices  490 us (65%)
  blocking collectives  110 us (15%)
  matrix products  86 us (11%)
  other arithmetic  22.3 us (3%)
  local copies, waits for them, and re-layouts  20.8 us (3%)
  between operations  17.6 us (2%)
    unnamed x20, waiting for transfers between devices  109 us
    all_gather x4, waiting for transfers between devices, gather_rows(): return lax.all_gather(local, 'tensor', axis=1, tiled=True)  108 us
    dot_general x18, matrix products, mat_dot(): return jnp.dot(left, right, preferred_element_type=jnp.float32)  68.7 us
    reduce_scatter x1, waiting for transfers between devices, shards(): lax.psum_scatter(up_grad, 'dp', scatter_dimension=0, tiled=True)  61.1 us
    reduce_scatter x1, waiting for transfers between devices, shards(): lax.psum_scatter(query_grad, 'dp', scatter_dimension=0, tiled=True)  43.3 us
    reduce_scatter x1, waiting for transfers between devices, shards(): lax.psum_scatter(key_grad, 'dp', scatter_dimension=0, tiled=True)  43.1 us
    reduce_scatter x1, waiting for transfers between devices, shards(): lax.psum_scatter(value_grad, 'dp', scatter_dimension=0, tiled=True)  43.1 us
    reduce_scatter x1, waiting for transfers between devices, shards(): lax.psum_scatter(out_grad, 'dp', scatter_dimension=1, tiled=True)  43.1 us
  transfers between devices with their start and end apart: 16, of which 14 were waited for; matrix products, arithmetic and copies ran while one was open for 8% of the time, Pallas kernels for 0%

commit v1 on v0

--- a/solution.py
+++ b/solution.py
@@ -9,6 +9,9 @@
 EPSILON = 1e-06
 GELU_COEF = 0.7978845608028654
 MASK_FILL = -1e30
+manage_side = lambda packet, device_axis, ax_name: lax.psum(
+    lax.psum(packet, device_axis), axis_name=ax_name
+)
 
 
 def norm_forward(inputs, gain_vec, shift_vec):
@@ -243,7 +246,7 @@
     up_bias_full = lax.dynamic_update_slice_in_dim(
         jnp.zeros((up_bias_all.shape[0],), jnp.float32), up_bias_part, tensor_index * hidden_cols, 0
     )
-    vector_sums = lax.psum(
+    vector_sums = manage_side(
         (
             first_gain_grad,
             first_shift_grad,
@@ -255,7 +258,8 @@
             up_bias_full,
             down_bias_grad,
         ),
-        ("dp", "tensor"),
+        "tensor",
+        "dp",
     )
     vector_parts = tuple((vector_share(member, dp_count, dp_index) for member in vector_sums))
     return (output, input_grad) + tuple(matrix_shares) + vector_parts

time: 754 us -> 754 us (level)
    psum x1 -> x2, blocking collectives: 41.8 us -> 43.4 us  [the longest x1 24.7 us: lax.psum(lax.psum(packet, device_axis), axis_name=ax_name)]
where the time goes in v1:
time: 754 us; the launch traced here: 749 us
  waiting for transfers between devices  489 us (65%)
  blocking collectives  112 us (15%)
  matrix products  86 us (11%)
  other arithmetic  22.3 us (3%)
  local copies, waits for them, and re-layouts  20.8 us (3%)
  between operations  17.6 us (2%)
    unnamed x20, waiting for transfers between devices  109 us
    all_gather x4, waiting for transfers between devices, gather_rows(): return lax.all_gather(local, 'tensor', axis=1, tiled=True)  108 us
    dot_general x18, matrix products, mat_dot(): return jnp.dot(left, right, preferred_element_type=jnp.float32)  68.7 us
    reduce_scatter x1, waiting for transfers between devices, shards(): lax.psum_scatter(up_grad, 'dp', scatter_dimension=0, tiled=True)  61 us
    reduce_scatter x1, waiting for transfers between devices, shards(): lax.psum_scatter(query_grad, 'dp', scatter_dimension=0, tiled=True)  43.3 us
    reduce_scatter x1, waiting for transfers between devices, shards(): lax.psum_scatter(value_grad, 'dp', scatter_dimension=0, tiled=True)  43.1 us
    reduce_scatter x1, waiting for transfers between devices, shards(): lax.psum_scatter(key_grad, 'dp', scatter_dimension=0, tiled=True)  43.1 us
    reduce_scatter x1, waiting for transfers between devices, shards(): lax.psum_scatter(out_grad, 'dp', scatter_dimension=1, tiled=True)  43.1 us
  transfers between devices with their start and end apart: 16, of which 14 were waited for; matrix products, arithmetic and copies ran while one was open for 8% of the time, Pallas kernels for 0%

profile of v1, /device:TPU:0, one launch (start us, length us, event | category | flops | bytes accessed | tf_op | source)
XLA Modules:
  0.0 748.9 jit_solution(6385166101310155519)
XLA Ops:
  20.8 26.1 %all-reduce.15 = (bf16[1152]{0:T(1024)(128)(2,1)S(1)}, bf16[1152]{0:T(1024)(128)(2,1)S(1)}, bf16[1152]{0:T(1024)(128)(2,1)S(1)}, bf16[1152]{0:T(1024)(128)(2,1)S...) all-reduce(bf16[1152]{0:T(1024)(128)(2,1)S(1)} %dynamic-update-slic, ...), channel_id=1, replica_groups=mesh['dp'=8,'tensor'=4] {'dp'}, use_global_device_ids=true, to_apply=%add.6 | all-reduce | flops 13520 | bytes 54080
  49.9 10.0 %all_gather.68 = bf16[1152,288]{1,0:T(8,128)(2,1)S(1)} all-gather(bf16[144,288]{1,0:T(8,128)(2,1)} %param.20), channel_id=1, replica_groups=mesh['dp'=8,'tensor'=4] {'dp'}, dimensions={0}, use_global_device_ids=true | all-gather | bytes 746496 | tf_op jit(solution)/shard_map/all_gather | solution.py:120
  59.9 10.5 %all_gather.70 = bf16[1152,288]{1,0:T(8,128)(2,1)S(1)} all-gather(bf16[144,288]{1,0:T(8,128)(2,1)S(1)} %copy-done.18), channel_id=1, replica_groups=mesh['dp'=8,'tensor'=4] {'dp'}, dimensions={0}, use_global_device_ids=true | all-gather | bytes 746496 | tf_op jit(solution)/shard_map/all_gather | solution.py:121
  70.4 10.2 %all_gather.66 = bf16[1152,288]{1,0:T(8,128)(2,1)S(1)} all-gather(bf16[144,288]{1,0:T(8,128)(2,1)S(1)} %copy-done.19), channel_id=1, replica_groups=mesh['dp'=8,'tensor'=4] {'dp'}, dimensions={0}, use_global_device_ids=true | all-gather | bytes 746496 | tf_op jit(solution)/shard_map/all_gather | solution.py:122
  80.5 11.5 %all_gather.71 = bf16[288,1152]{0,1:T(8,128)(2,1)} all-gather(bf16[288,144]{0,1:T(8,128)(2,1)S(1)} %copy-done.20), channel_id=1, replica_groups=mesh['dp'=8,'tensor'=4] {'dp'}, dimensions={1}, use_global_device_ids=true | all-gather | bytes 746496 | tf_op jit(solution)/shard_map/all_gather | solution.py:123
  106.2 37.0 %reduce-scatter.35.cloned.1.call-done = bf16[1,184,1152]{2,1,0:T(8,128)(2,1)} async-done(((bf16[1,736,1152]{2,1,0:T(8,128)(2,1)}), bf16[1,184,1152]{2,1,0:T(8,128)(2,1)}) %reduce-scatter.35.cloned.1.call-update) | async-done | bytes 423952
  149.5 36.8 %all-gather.9.cloned.1.call-done = bf16[1,736,1152]{2,1,0:T(8,128)(2,1)} async-done(((bf16[1,184,1152]{2,1,0:T(8,128)(2,1)}), bf16[1,736,1152]{2,1,0:T(8,128)(2,1)}) %all-gather.9.cloned.1.call-update) | async-done | bytes 1695760 | tf_op jit(solution)/shard_map/all_gather | solution.py:47
  186.3 6.4 convolution_add_fusion.2
  192.8 32.8 %all-gather.15.cloned.1.call-done = bf16[1,736,1152]{2,1,0:T(8,128)(2,1)} async-done(((bf16[1,184,1152]{2,1,0:T(8,128)(2,1)}), bf16[1,736,1152]{2,1,0:T(8,128)(2,1)}) %all-gather.15.cloned.1.call-update) | async-done | bytes 1695760 | tf_op jit(solution)/shard_map/all_gather | solution.py:47
  225.6 30.9 %all-gather.13.cloned.1.call-done = bf16[1076,1152]{0,1:T(8,128)(2,1)} async-done(((bf16[1076,144]{0,1:T(8,128)(2,1)}), bf16[1076,1152]{0,1:T(8,128)(2,1)}) %all-gather.13.cloned.1.call-update) | async-done | bytes 2479120 | tf_op jit(solution)/shard_map/all_gather | solution.py:125
  256.5 8.2 %fusion.86 = (f32[1076]{0:T(1024)}, bf16[736,1076]{0,1:T(8,128)(2,1)S(1)}) fusion(f32[736,1076]{0,1:T(8,128)} %convolution_add_fusion.2, bf16[1076,1152]{0,1:T(8,128)(2,1)} %all-gather.13.cloned.1.call-done, bf16[1,736,1152]{2,1,0:T(8,128)(2,1)} %all-gather.15.cloned.1.call-done), kind=kOutput, calls=%fused_computation.117 | convolution fusion | flops 1840458240 | bytes 8930768 | tf_op jit(solution)/shard_map/dot_general | solution.py:43
  265.9 4.0 fusion.8
  269.9 7.2 fusion.7
  277.2 30.1 %reduce-scatter.39.cloned.1.call-done = bf16[1,184,1152]{2,1,0:T(8,128)(2,1)} async-done(((bf16[1,736,1152]{2,1,0:T(8,128)(2,1)}), bf16[1,184,1152]{2,1,0:T(8,128)(2,1)}) %reduce-scatter.39.cloned.1.call-update) | async-done | bytes 423952
  309.5 36.8 %reduce-scatter.37.cloned.1.call-done = bf16[1,184,1152]{2,1,0:T(8,128)(2,1)} async-done(((bf16[1,736,1152]{2,1,0:T(8,128)(2,1)}), bf16[1,184,1152]{2,1,0:T(8,128)(2,1)}) %reduce-scatter.37.cloned.1.call-update) | async-done | bytes 423952
  350.2 38.2 %all-gather.17.cloned.1.call-done = bf16[1,736,1152]{2,1,0:T(8,128)(2,1)} async-done(((bf16[1,184,1152]{2,1,0:T(8,128)(2,1)}), bf16[1,736,1152]{2,1,0:T(8,128)(2,1)}) %all-gather.17.cloned.1.call-update) | async-done | bytes 1695760 | tf_op jit(solution)/shard_map/all_gather | solution.py:47
  392.1 5.6 fusion.84
  397.8 5.6 multiply_convert_fusion
  410.8 7.4 fusion.15
  419.7 6.5 fusion.18
  427.2 3.9 fusion.11
  431.2 3.9 fusion.21
  435.2 3.9 fusion.25
  439.2 3.8 fusion.23
  448.2 18.7 %all-reduce.14 = (f32[1152]{0:T(1024)S(1)}, f32[1152]{0:T(1024)S(1)}, f32[1152]{0:T(1024)S(1)}, f32[1152]{0:T(1024)S(1)}, f32[1152]{0:T(1024)S(1)}, /*index=5*/f...) all-reduce(f32[1152]{0:T(1024)S(1)} %get-tuple-element.73, ...), channel_id=1, replica_groups=mesh['dp'=8,'tensor'=4] {'tensor'}, use_global_device_ids=true, to_apply=%region_22.23 | all-reduce | flops 13520 | bytes 108160 | tf_op jit(solution)/shard_map/psum | solution.py:13
  466.9 24.7 %all-reduce.13 = (f32[1152]{0:T(1024)S(1)}, f32[1152]{0:T(1024)S(1)}, f32[1152]{0:T(1024)S(1)}, f32[1152]{0:T(1024)S(1)}, f32[1152]{0:T(1024)S(1)}, /*index=5*/f...) all-reduce(f32[1152]{0:T(1024)S(1)} %get-tuple-element.88, ...), channel_id=1, replica_groups=mesh['dp'=8,'tensor'=4] {'dp'}, use_global_device_ids=true, to_apply=%region_23.24 | all-reduce | flops 13520 | bytes 108160 | tf_op jit(solution)/shard_map/psum | solution.py:12
  499.6 8.2 %reduce-scatter.33.cloned.1.call-done = f32[1076,144]{0,1:T(8,128)} async-done(((f32[1076,1152]{0,1:T(8,128)}), f32[1076,144]{0,1:T(8,128)}) %reduce-scatter.33.cloned.1.call-update) | async-done | bytes 619792 | tf_op jit(solution)/shard_map/reduce_scatter | solution.py:238
  507.8 61.0 %reduce-scatter.31.cloned.1.call-done = f32[144,1076]{1,0:T(8,128)} async-done(((f32[1152,1076]{1,0:T(8,128)}), f32[144,1076]{1,0:T(8,128)}) %reduce-scatter.31.cloned.1.call-update) | async-done | bytes 619792 | tf_op jit(solution)/shard_map/reduce_scatter | solution.py:237
  568.8 43.1 %reduce-scatter.29.cloned.1.call-done = f32[288,144]{0,1:T(8,128)} async-done(((f32[288,1152]{0,1:T(8,128)}), f32[288,144]{0,1:T(8,128)}) %reduce-scatter.29.cloned.1.call-update) | async-done | bytes 165904 | tf_op jit(solution)/shard_map/reduce_scatter | solution.py:236
  611.9 43.1 %reduce-scatter.27.cloned.1.call-done = f32[144,288]{1,0:T(8,128)} async-done(((f32[1152,288]{1,0:T(8,128)}), f32[144,288]{1,0:T(8,128)}) %reduce-scatter.27.cloned.1.call-update) | async-done | bytes 165904 | tf_op jit(solution)/shard_map/reduce_scatter | solution.py:235
  655.0 43.3 %reduce-scatter.23.cloned.1.call-done = f32[144,288]{1,0:T(8,128)} async-done(((f32[1152,288]{1,0:T(8,128)}), f32[144,288]{1,0:T(8,128)}) %reduce-scatter.23.cloned.1.call-update) | async-done | bytes 165904 | tf_op jit(solution)/shard_map/reduce_scatter | solution.py:233
  698.3 43.1 %reduce-scatter.25.cloned.1.call-done = f32[144,288]{1,0:T(8,128)} async-done(((f32[1152,288]{1,0:T(8,128)}), f32[144,288]{1,0:T(8,128)}) %reduce-scatter.25.cloned.1.call-update) | async-done | bytes 165904 | tf_op jit(solution)/shard_map/reduce_scatter | solution.py:234
  (174 shorter events, 68.8 us)
Async XLA Ops:
  8.0 51.8 %copy-start.18 = (bf16[144,288]{1,0:T(8,128)(2,1)S(1)}, bf16[144,288]{1,0:T(8,128)(2,1)}, u32[]{:S(2)}) copy-start(bf16[144,288]{1,0:T(8,128)(2,1)} %param.21) | copy-start | bytes 248836
  8.0 62.3 %copy-start.19 = (bf16[144,288]{1,0:T(8,128)(2,1)S(1)}, bf16[144,288]{1,0:T(8,128)(2,1)}, u32[]{:S(2)}) copy-start(bf16[144,288]{1,0:T(8,128)(2,1)} %param.22) | copy-start | bytes 248836
  8.0 72.5 %copy-start.20 = (bf16[288,144]{0,1:T(8,128)(2,1)S(1)}, bf16[288,144]{0,1:T(8,128)(2,1)}, u32[]{:S(2)}) copy-start(bf16[288,144]{0,1:T(8,128)(2,1)} %param.23) | copy-start | bytes 248836
  8.1 84.0 %all-gather.7.cloned.1.call-start = ((), (), s32[]{:S(2)}) async-start(), calls=%async_computation.10 | async-start | bytes 2119680 | tf_op jit(solution)/shard_map/all_gather | solution.py:47
  48.9 94.3 %reduce-scatter.35.cloned.1.call-start = ((), (), s32[]{:S(2)}) async-start(), calls=%async_computation.22 | async-start | bytes 2119680
  70.4 24.9 %copy-start.3 = (bf16[1152,288]{1,0:T(8,128)(2,1)}, bf16[1152,288]{1,0:T(8,128)(2,1)S(1)}, u32[]{:S(2)}) copy-start(bf16[1152,288]{1,0:T(8,128)(2,1)S(1)} %all_gather.70) | copy-start | bytes 1990660
  98.8 3.5 copy-start.21
  102.3 40.9 %copy-start = (bf16[1,184,1152]{2,1,0:T(8,128)(2,1)S(1)}, bf16[1,184,1152]{2,1,0:T(8,128)(2,1)}, u32[]{:S(2)}) copy-start(bf16[1,184,1152]{2,1,0:T(8,128)(2,1)} %param.18) | copy-start | bytes 1271812
  105.5 44.0 %all-gather.11.cloned.1.call-start = ((), (), s32[]{:S(2)}) async-start(), calls=%async_computation.12 | async-start | bytes 2985984 | tf_op jit(solution)/shard_map/all_gather | solution.py:124
  106.1 80.2 %all-gather.9.cloned.1.call-start = ((), (), s32[]{:S(2)}) async-start(), calls=%async_computation.11 | async-start | bytes 2119680 | tf_op jit(solution)/shard_map/all_gather | solution.py:47
  147.8 77.8 %all-gather.15.cloned.1.call-start = ((), (), s32[]{:S(2)}) async-start(), calls=%async_computation.14 | async-start | bytes 2119680 | tf_op jit(solution)/shard_map/all_gather | solution.py:47
  148.4 108.1 %all-gather.13.cloned.1.call-start = ((), (), s32[]{:S(2)}) async-start(), calls=%async_computation.13 | async-start | bytes 2985984 | tf_op jit(solution)/shard_map/all_gather | solution.py:125
  149.1 158.2 %reduce-scatter.39.cloned.1.call-start = ((), (), s32[]{:S(2)}) async-start(), calls=%async_computation.24 | async-start | bytes 2119680
  256.5 9.4 %copy-start.24 = (bf16[1152,1076]{1,0:T(8,128)(2,1)S(1)}, bf16[1152,1076]{1,0:T(8,128)(2,1)}, u32[]{:S(2)}) copy-start(bf16[1152,1076]{1,0:T(8,128)(2,1)} %all-gather.11.cloned.1.call-done) | copy-start | bytes 7437316
  269.9 37.4 %copy-start.2 = (bf16[1,184,1152]{2,1,0:T(8,128)(2,1)S(1)}, bf16[1,184,1152]{2,1,0:T(8,128)(2,1)}, u32[]{:S(2)}) copy-start(bf16[1,184,1152]{2,1,0:T(8,128)(2,1)} %reduce-scatter.35.cloned.1.call-done) | copy-start | bytes 1271812
  269.9 76.4 %reduce-scatter.37.cloned.1.call-start = ((), (), s32[]{:S(2)}) async-start(), calls=%async_computation.23 | async-start | bytes 2119680
  277.2 111.3 %all-gather.17.cloned.1.call-start = ((), (), s32[]{:S(2)}) async-start(), calls=%async_computation.15 | async-start | bytes 2119680 | tf_op jit(solution)/shard_map/all_gather | solution.py:47
  348.9 43.2 %copy-start.22 = (f32[4,736]{1,0:T(4,128)S(1)}, f32[4,736]{1,0:T(4,128)}, u32[]{:S(2)}) copy-start(f32[4,736]{1,0:T(4,128)} %copy-done.21) | copy-start | bytes 35332
  349.8 96.9 %reduce-scatter.41.cloned.1.call-start = ((), (), s32[]{:S(2)}) async-start(), calls=%async_computation.25 | async-start | bytes 2119680
  392.1 5.7 copy-start.28
  397.8 10.6 %copy-start.14 = (bf16[736,4,72]{0,2,1:T(8,128)(2,1)}, bf16[736,4,72]{0,2,1:T(8,128)(2,1)S(1)}, u32[]{:S(2)}) copy-start(bf16[736,4,72]{0,2,1:T(8,128)(2,1)S(1)} %get-tuple-element.109) | copy-start | bytes 1271812
  397.8 5.6 copy-start.10
  410.8 97.0 %reduce-scatter.33.cloned.1.call-start = ((), (), s32[]{:S(2)}) async-start(), calls=%async_computation.21 | async-start | bytes 5971968 | tf_op jit(solution)/shard_map/reduce_scatter | solution.py:238
  418.2 150.6 %reduce-scatter.31.cloned.1.call-start = ((), (), s32[]{:S(2)}) async-start(), calls=%async_computation.20 | async-start | bytes 5971968 | tf_op jit(solution)/shard_map/reduce_scatter | solution.py:237
  426.2 5.0 copy-start.15
  426.2 185.7 %reduce-scatter.29.cloned.1.call-start = ((), (), s32[]{:S(2)}) async-start(), calls=%async_computation.19 | async-start | bytes 1990656 | tf_op jit(solution)/shard_map/reduce_scatter | solution.py:236
  431.1 4.1 copy-start.6
  431.1 223.9 %reduce-scatter.27.cloned.1.call-start = ((), (), s32[]{:S(2)}) async-start(), calls=%async_computation.18 | async-start | bytes 1990656 | tf_op jit(solution)/shard_map/reduce_scatter | solution.py:235
  435.1 4.1 copy-start.12
  435.1 263.1 %reduce-scatter.23.cloned.1.call-start = ((), (), s32[]{:S(2)}) async-start(), calls=%async_computation.16 | async-start | bytes 1990656 | tf_op jit(solution)/shard_map/reduce_scatter | solution.py:233
  439.1 3.9 copy-start.23
  439.1 302.3 %reduce-scatter.25.cloned.1.call-start = ((), (), s32[]{:S(2)}) async-start(), calls=%async_computation.17 | async-start | bytes 1990656 | tf_op jit(solution)/shard_map/reduce_scatter | solution.py:234
  (14 other events, 26.0 us)
Sparse Core Ops, SparseCore 0:
  49.1 38.4 all-gather.6
  105.7 37.5 reduce-scatter.34
  270.0 37.2 reduce-scatter.38
  309.5 36.7 reduce-scatter.36
  349.9 38.5 all-gather.16
Sparse Core Ops, SparseCore 1:
  107.9 30.3 all-gather.10
  147.9 38.4 all-gather.8
  187.8 37.8 all-gather.14
  227.5 28.9 all-gather.12
  410.9 35.8 reduce-scatter.40
  450.7 57.0 reduce-scatter.32
  512.0 56.7 reduce-scatter.30
  572.6 39.2 reduce-scatter.28
  615.7 39.2 reduce-scatter.26
  659.0 39.2 reduce-scatter.22
  702.1 39.2 reduce-scatter.24
